TPU v7x, 256 devices: a whole 4x4x8 slice. The times are simulated.
256 devices in a mesh: row: 32 (over z_lo, x, core), col: 8 (over z_hi, y).
Axes of the slice: x: 4, y: 4, z: 8 (z_hi: 2, z_lo: 4; z = z_hi * 4 + z_lo), core: 2. Of those that a mesh axis runs over, the one named last changes fastest.
Arguments:
- activations: bfloat16 [1024, 16384], P('col', 'row'), may hold values from 0 to 2
- blocks_one: bfloat16 [32, 8, 64, 128, 128], P('row', 'col'), may hold values from -0.09375 to 0.09375
- pattern_one: int32 [32, 8, 64], P('row', 'col'), may hold values from 0 to 63, as said below
- count_one: int32 [32, 8], P('row', 'col'), may hold values from 1 to 64, as said below
- blocks_two: bfloat16 [8, 32, 64, 128, 128], P('col', 'row'), may hold values from -0.125 to 0.125
- pattern_two: int32 [8, 32, 64], P('col', 'row'), may hold values from 0 to 63, as said below
- count_two: int32 [8, 32], P('col', 'row'), may hold values from 1 to 64, as said below
Outputs:
- sparse_out: bfloat16 [1024, 16384], P('col', 'row')
Inputs may be any that keep to these rules, and one draw needn't show every extreme that they name: `pattern_one`: in each tile the slots below its count hold distinct positions; slots at or above the count hold positions in range whose blocks are not part of the weights. `count_one`: some tile has exactly 64 live slots. `pattern_two`: in each tile the slots below its count hold distinct positions; slots at or above the count hold positions in range whose blocks are not part of the weights. `count_two`: some tile has exactly 64 live slots.
All inputs are finite; a program needn't handle non-finite values.
Results may differ from a plain program's by a relative error of at most 0.0053.
Values may be sent and summed in bfloat16 or wider, within the bound.
A program may use at most 64 MiB of HBM per device.

v0:
```python
import jax
import jax.numpy as jnp
from jax import lax
from jax.sharding import Mesh
from jax.sharding import PartitionSpec as P

N = 16384
ROW = ("row_0", "row_1", "row_2")


bias_value = -0.3


def from_everyone(array, axis):
    copies = jnp.broadcast_to(array, (lax.axis_size(axis), *array.shape))
    return lax.all_to_all(copies, axis, split_axis=0, concat_axis=0, tiled=True)


def joined_along(pieces, dim):
    pieces = jnp.moveaxis(pieces, 0, dim)
    shape = pieces.shape
    return pieces.reshape(*shape[:dim], shape[dim] * shape[dim + 1], *shape[dim + 2 :])


def gather_directly(array, axis, dim):
    pieces = from_everyone(array, axis)
    return joined_along(pieces, dim)


def split_up(array, dim, devices):
    before, after = (array.shape[:dim], array.shape[dim + 1 :])
    return jnp.moveaxis(array.reshape(*before, devices, -1, *after), dim, 0)


def scatter_pairs(array, chips, core, dim):
    sizes = (lax.axis_size(chips), lax.axis_size(core))
    pieces = split_up(array, dim, sizes[0] * sizes[1])
    inside = pieces.shape[1:]
    pieces = pieces.reshape(*sizes, *inside).swapaxes(0, 1).reshape(-1, *inside)
    pieces = lax.psum_scatter(pieces, core, scatter_dimension=0, tiled=True)
    return lax.psum_scatter(pieces, chips, scatter_dimension=0, tiled=True)[0]


def sum_at_owner(array, axis, dim):
    devices = lax.axis_size(axis)
    pieces = lax.all_to_all(split_up(array, dim, devices), axis, 0, 0, tiled=True)
    return jnp.sum(pieces, axis=0)


def build_tile(where, live, blocks, block_rows, block_cols):
    slots = blocks.shape[0]
    size = blocks.shape[-1]
    places = jnp.arange(block_rows * block_cols, dtype=jnp.int32)
    used = jnp.arange(slots, dtype=jnp.int32) < live
    onehot = ((places[:, None] == where[None, :]) & used[None, :]).astype(jnp.bfloat16)
    flat = blocks.reshape(slots, size * size)
    tiles = jnp.dot(onehot, flat, preferred_element_type=jnp.float32).astype(jnp.bfloat16)
    tiles = tiles.reshape(block_rows, block_cols, size, size).transpose(0, 2, 1, 3)
    return tiles.reshape(block_rows * size, block_cols * size)


def apply_blocks(panel, where, live, blocks, width):
    size = blocks.shape[-1]
    block_rows = panel.shape[1] // size
    block_cols = width // size
    tile = build_tile(where, live, blocks, block_rows, block_cols)
    return jnp.dot(panel, tile, preferred_element_type=jnp.float32)


def shards(activations, blocks_one, pattern_one, count_one, blocks_two, pattern_two, count_two):
    where_one = pattern_one.reshape(-1)
    live_one = count_one.reshape(())
    stored_one = blocks_one.reshape(blocks_one.shape[2:])
    where_two = pattern_two.reshape(-1)
    live_two = count_two.reshape(())
    stored_two = blocks_two.reshape(blocks_two.shape[2:])
    width_one = N // lax.axis_size("col")
    width_two = N // lax.axis_size(ROW)
    partial_one = apply_blocks(
        gather_directly(activations, "col", 0), where_one, live_one, stored_one, width_one
    )
    share = scatter_pairs(partial_one, ("row_0", "row_1"), "row_2", 0)
    hidden_share = jnp.maximum(share + bias_value, 0.0).astype(jnp.bfloat16)
    partial_two = apply_blocks(
        lax.all_gather(hidden_share, ROW, axis=0, tiled=True),
        where_two,
        live_two,
        stored_two,
        width_two,
    )
    result = sum_at_owner(partial_two, "col", 0)
    return jnp.maximum(result + bias_value, 0.0).astype(jnp.bfloat16)


def solution(mesh):
    split = Mesh(
        mesh.devices.reshape(4, 4, 2, mesh.shape["col"]), ("row_0", "row_1", "row_2", "col")
    )
    return jax.shard_map(
        shards,
        mesh=split,
        in_specs=(
            P("col", ROW),
            P(ROW, "col", None, None, None),
            P(ROW, "col", None),
            P(ROW, "col"),
            P("col", ROW, None, None, None),
            P("col", ROW, None),
            P("col", ROW),
        ),
        out_specs=P("col", ROW),
        check_vma=False,
    )
```

profile of v0, /device:TPU:32, one launch (start us, length us, event | category | flops | bytes accessed | tf_op | source)
XLA Modules:
  0.0 306.1 jit_solution(11263311072547643464)
XLA Ops:
  6.5 0.0 copy-start.2
  6.5 0.0 copy-start
  6.5 2.1 broadcast_in_dim.2
  8.7 10.2 %all-to-all-start = ((bf16[8,128,512]{2,1,0:T(8,128)(2,1)}), bf16[8,128,512]{2,1,0:T(8,128)(2,1)S(1)}, u32[]{:S(2)}, u32[]{:S(2)}) async-start(bf16[8,128,512]{2,1,0:T(8,128)(2,1)} %broadcast_in_dim.2), calls=%async_computation | async-start | bytes 2097152 | tf_op jit(solution)/shard_map/all_to_all | solution.py:16
  18.9 0.0 reduce-scatter.3.cloned.1.call-start
  19.6 0.0 copy-done.2
  19.6 0.0 copy-done
  19.6 1.7 fusion.7
  21.3 0.6 copy.13
  21.9 1.4 copy.9
  23.2 24.7 %all-to-all-done = bf16[8,128,512]{2,1,0:T(8,128)(2,1)S(1)} async-done(((bf16[8,128,512]{2,1,0:T(8,128)(2,1)}), bf16[8,128,512]{2,1,0:T(8,128)(2,1)S(1)}, u32[]{:S(2)}, u32[]{:S(2)}) %all-to-all-start) | async-done | bytes 1048608 | tf_op jit(solution)/shard_map/all_to_all | solution.py:16
  47.9 2.3 fusion.2
  50.3 3.8 %copy.10 = f32[16,2,32,2048]{3,2,0,1:T(8,128)} copy(f32[16,2,32,2048]{3,2,1,0:T(8,128)S(1)} %bitcast.48) | data formatting | bytes 16777216 | tf_op jit(solution)/shard_map/reshape;reshape | solution.py:39
  54.1 0.0 reduce-scatter.3.cloned.1.call-update
  54.1 0.0 reduce-scatter.5.cloned.1.call-start
  54.2 19.5 %reduce-scatter.3.cloned.1.call-done = f32[16,32,2048]{2,1,0:T(8,128)} async-done(((f32[32,32,2048]{2,1,0:T(8,128)}), f32[16,32,2048]{2,1,0:T(8,128)}) %reduce-scatter.3.cloned.1.call-update) | async-done | bytes 4194320 | tf_op jit(solution)/shard_map/reduce_scatter | solution.py:40
  73.7 0.0 reduce-scatter.5.cloned.1.call-update
  73.7 0.0 all-gather.3.cloned.1.call-start
  73.8 90.5 %reduce-scatter.5.cloned.1.call-done = f32[1,32,2048]{2,1,0:T(8,128)} async-done(((f32[16,32,2048]{2,1,0:T(8,128)}), f32[1,32,2048]{2,1,0:T(8,128)}) %reduce-scatter.5.cloned.1.call-update) | async-done | bytes 262160 | tf_op jit(solution)/shard_map/reduce_scatter | solution.py:41
  164.3 1.6 maximum_convert_fusion.1
  165.9 0.0 all-gather.3.cloned.1.call-update
  166.6 0.0 copy-done.1
  166.6 0.0 copy-done.3
  166.6 1.7 fusion.10
  168.3 0.6 copy.16
  168.9 1.8 copy.11
  170.7 2.2 reshape.51
  172.9 59.4 %all-gather.3.cloned.1.call-done = bf16[1,1024,2048]{2,1,0:T(8,128)(2,1)} async-done(((bf16[1,32,2048]{2,1,0:T(8,128)(2,1)}), bf16[1,1024,2048]{2,1,0:T(8,128)(2,1)}) %all-gather.3.cloned.1.call-update) | async-done | bytes 4194320 | tf_op jit(solution)/shard_map/all_gather | solution.py:85
  232.3 5.2 %fusion.21 = f32[8,128,512]{2,1,0:T(8,128)S(1)} fusion(bf16[8,128,2048]{2,1,0:T(8,128)(2,1)} %bitcast.57, bf16[2048,512,1]{1,0,2:T(8,128)(2,1)} %reshape.51), kind=kOutput, calls=%fused_computation.23 | convolution fusion | flops 2147483648 | bytes 8388608 | tf_op jit(solution)/shard_map/dot_general | solution.py:67
  237.5 61.1 %all_to_all.10 = f32[8,128,512]{2,1,0:T(8,128)S(1)} all-to-all(f32[8,128,512]{2,1,0:T(8,128)S(1)} %fusion.21), channel_id=1, replica_groups=mesh['row_0'=4,'row_1'=4,'row_2'=2,'col'=8] {'col'}, dimensions={0} | all-to-all | bytes 4194304 | tf_op jit(solution)/shard_map/all_to_all | solution.py:46
  298.7 0.2 reduce_sum.9
  298.9 0.7 maximum_convert_fusion
  (4 shorter events, 0.0 us)
Async XLA Ops:
  6.5 13.0 %copy-start.2 = (s32[1,1,64]{2,1,0:T(1,128)S(1)}, s32[1,1,64]{2,1,0:T(1,128)}, u32[]{:S(2)}) copy-start(s32[1,1,64]{2,1,0:T(1,128)} %param.9) | copy-start | bytes 772
  6.5 13.0 %copy-start = (bf16[1,1,64,128,128]{4,3,2,1,0:T(8,128)(2,1)S(1)}, bf16[1,1,64,128,128]{4,3,2,1,0:T(8,128)(2,1)}, u32[]{:S(2)}) copy-start(bf16[1,1,64,128,128]{4,3,2,1,0:T(8,128)(2,1)} %param.8) | copy-start | bytes 6291460
  8.7 39.3 %all-to-all-start = ((bf16[8,128,512]{2,1,0:T(8,128)(2,1)}), bf16[8,128,512]{2,1,0:T(8,128)(2,1)S(1)}, u32[]{:S(2)}, u32[]{:S(2)}) async-start(bf16[8,128,512]{2,1,0:T(8,128)(2,1)} %broadcast_in_dim.2), calls=%async_computation | async-start | bytes 2097152 | tf_op jit(solution)/shard_map/all_to_all | solution.py:16
  18.9 54.8 %reduce-scatter.3.cloned.1.call-start = ((), (), s32[]{:S(2)}) async-start(), calls=%async_computation.4 | async-start | bytes 12582912 | tf_op jit(solution)/shard_map/reduce_scatter | solution.py:40
  54.1 110.1 %reduce-scatter.5.cloned.1.call-start = ((), (), s32[]{:S(2)}) async-start(), calls=%async_computation.5 | async-start | bytes 4456448 | tf_op jit(solution)/shard_map/reduce_scatter | solution.py:41
  73.7 92.9 %copy-start.1 = (bf16[1,1,64,128,128]{4,3,2,1,0:T(8,128)(2,1)S(1)}, bf16[1,1,64,128,128]{4,3,2,1,0:T(8,128)(2,1)}, u32[]{:S(2)}) copy-start(bf16[1,1,64,128,128]{4,3,2,1,0:T(8,128)(2,1)} %param.11) | copy-start | bytes 6291460
  73.7 92.9 %copy-start.3 = (s32[1,1,64]{2,1,0:T(1,128)S(1)}, s32[1,1,64]{2,1,0:T(1,128)}, u32[]{:S(2)}) copy-start(s32[1,1,64]{2,1,0:T(1,128)} %param.12) | copy-start | bytes 772
  73.7 158.6 %all-gather.3.cloned.1.call-start = ((), (), s32[]{:S(2)}) async-start(), calls=%async_computation.6 | async-start | bytes 4325376 | tf_op jit(solution)/shard_map/all_gather | solution.py:85
Sparse Core Ops, SparseCore 0:
  54.2 19.4 reduce-scatter.2
  76.4 87.8 reduce-scatter.4
  166.3 65.9 all-gather.2
where the time goes:
time: 306 us
  waiting for transfers between devices  194 us (63%)
  blocking collectives  61.1 us (20%)
  between operations  14.5 us (5%)
  local copies, waits for them, and re-layouts  12.4 us (4%)
  matrix products  10.9 us (4%)
  starting transfers between devices  10.3 us (3%)
    reduce_scatter x1, waiting for transfers between devices, scatter_pairs(): return lax.psum_scatter(pieces, chips, scatter_dimension=0, tiled=True)[0]  90.5 us
    all_to_all x1, blocking collectives, sum_at_owner(): lax.all_to_all(split_up(array, dim, devices), axis, 0, 0, tiled=True)  61.1 us
    all_gather x1, waiting for transfers between devices, shards(): lax.all_gather(hidden_share, ROW, axis=0, tiled=True)  59.4 us
    all_to_all x1, waiting for transfers between devices, from_everyone(): return lax.all_to_all(copies, axis, split_axis=0, concat_axis=0, tiled=True)  24.7 us
    reduce_scatter x1, waiting for transfers between devices, scatter_pairs(): pieces = lax.psum_scatter(pieces, core, scatter_dimension=0, tiled=True)  19.5 us
    all_to_all x1, starting transfers between devices, from_everyone(): return lax.all_to_all(copies, axis, split_axis=0, concat_axis=0, tiled=True)  10.2 us
    dot_general x2, matrix products, apply_blocks(): return jnp.dot(panel, tile, preferred_element_type=jnp.float32)  7.53 us
  transfers between devices with their start and end apart: 4, of which 4 were waited for; matrix products, arithmetic and copies ran while one was open for 3% of the time, Pallas kernels for 0%

commit v1 on v0

v1 whole, which is shorter than its diff:
```python
import jax
import jax.numpy as jnp
from jax import lax
from jax.experimental import pallas as pl
from jax.experimental.pallas import tpu as pltpu
from jax.sharding import PartitionSpec as P

MESH = pl.DeviceIdType.MESH
BIAS = -0.3
BLK = 128
SLOTS = 64
ROWS = 128
WIDE = 2048
NARROW = 512
CHUNKS = 8
HALF, PIECE = ROWS // 2, ROWS // 8
ORDER = ((0, 1), (0, 3), (1, 0), (1, 1), (1, 3), (1, 2), (0, 2), (0, 0))
AT = {step: k for k, step in enumerate(ORDER)}
LAST_OTHER = max(AT[1, d] for d in range(4))
PLAN = (
    ("spread_core", 4),
    ("first", 0),
    ("sum_x", 1),
    ("second", 4),
    ("sum_core", 0),
    ("sum_z", 2),
    ("spread_x", 3),
    ("sum_other", 5),
)
Z_TYPE = jnp.bfloat16


def kernel(
    table, act, blocks_one, blocks_two, out,
    stored_one, stored_two, tile_one, tile_two, rows_in, part_one, core_in, x_out, x_in, x_own, z_sum, z_out, z_in, hidden,
    part_two, kept, y_out, y_in, zh_out, zh_in,
    load_sem, act_send, act_recv, core_send, core_recv, x_send, x_recv, z_send, z_recv,
    hz_send, hz_recv, hx_send, hx_recv, hc_send, hc_recv, y_send, y_recv, zh_send, zh_recv,
):
    row, col = lax.axis_index("row"), lax.axis_index("col")
    zl, x, core = row // 8, (row // 2) % 4, row % 2
    zh, y = col // 4, col % 4

    def row_at(zl, x, core):
        return ((zl * 4 + x) * 2 + core, col)

    other_core = row_at(zl, x, 1 - core)
    x_peer = [row_at(zl, (x + d) % 4, core) for d in range(4)]
    z_peer = [row_at((zl + d) % 4, x, core) for d in range(4)]
    y_peer = [(row, zh * 4 + (y + d) % 4) for d in range(4)]
    zh_peer = (row, (1 - zh) * 4 + y)

    def send(src, dst, send_sem, recv_sem, device):
        return pltpu.make_async_remote_copy(
            src_ref=src, dst_ref=dst, send_sem=send_sem, recv_sem=recv_sem,
            device_id=device, device_id_type=MESH,
        )

    def act_copy(src, k, device):
        return send(src, rows_in.at[k], act_send.at[k], act_recv.at[k], device)

    def core_copy(k):
        src = part_one.at[k, pl.ds(pl.multiple_of((1 - core) * HALF, HALF), HALF)]
        return send(src, core_in.at[k], core_send.at[k], core_recv.at[k], other_core)

    def x_copy(k, d):
        src = x_out.at[k, pl.ds(pl.multiple_of((x + d) % 4 * PIECE, PIECE), PIECE)]
        return send(src, x_in.at[k, d - 1], x_send.at[k, d - 1], x_recv.at[k, d - 1], x_peer[d])

    def z_copy(k, d):
        src = z_out.at[k, :, pl.ds(pl.multiple_of((zl + d) % 4 * NARROW, NARROW), NARROW)]
        return send(src, z_in.at[k, d - 1], z_send.at[k, d - 1], z_recv.at[k, d - 1], z_peer[d])

    mine = pl.ds(pl.multiple_of(core * HALF + x * PIECE, PIECE), PIECE)
    my_half = pl.ds(pl.multiple_of(core * HALF, HALF), HALF)
    my_cols = pl.ds(pl.multiple_of(zl * NARROW, NARROW), NARROW)

    def hz_copy(k, d):
        ref = hidden.at[k, mine, my_cols]
        return send(ref, ref, hz_send.at[k, d - 1], hz_recv.at[k, d - 1], z_peer[d])

    def hx_copy(k, d):
        ref = hidden.at[k, mine]
        return send(ref, ref, hx_send.at[k, d - 1], hx_recv.at[k, d - 1], x_peer[d])

    def hc_copy(k):
        ref = hidden.at[k, my_half]
        return send(ref, ref, hc_send.at[k], hc_recv.at[k], other_core)

    def y_copy(half, d):
        return send(
            y_out.at[half, d - 1], y_in.at[half, d - 1], y_send.at[half, d - 1], y_recv.at[half, d - 1], y_peer[d]
        )

    def zh_copy():
        return send(zh_out, zh_in, zh_send, zh_recv, zh_peer)

    def act_sends():
        yield act_copy(act, AT[1, 0], zh_peer)
        for d in (3, 1, 2):
            yield act_copy(act, AT[0, 4 - d], y_peer[d])

    def act_forwards():
        for d in (3, 1, 2):
            yield act_copy(rows_in.at[AT[1, 0]], AT[1, 4 - d], y_peer[d])

    loads = [
        pltpu.make_async_copy(ref, stored.at[pl.ds(0, SLOTS)], load_sem.at[layer])
        for layer, (ref, stored) in enumerate(((blocks_one, stored_one), (blocks_two, stored_two)))
    ]
    for load in loads:
        load.start()

    barrier = pltpu.get_barrier_semaphore()
    partners = [other_core, zh_peer, *x_peer[1:], *z_peer[1:], *y_peer[1:]]
    for device in partners:
        pl.semaphore_signal(barrier, inc=1, device_id=device, device_id_type=MESH)
    pl.semaphore_wait(barrier, len(partners))

    for copy in act_sends():
        copy.start()
    rows_in[AT[0, 0]] = act[...]
    for stored in (stored_one, stored_two):
        stored[SLOTS] = jnp.zeros((BLK, BLK), jnp.bfloat16)

    def build(layer, stored, tile, block_cols):
        def place(p, _):
            r = pl.multiple_of(p // block_cols * BLK, BLK)
            c = pl.multiple_of(p % block_cols * BLK, BLK)
            tile[pl.ds(r, BLK), pl.ds(c, BLK)] = stored[table[layer, p]]
            return 0

        loads[layer].wait()
        lax.fori_loop(0, SLOTS, place, 0)

    build(0, stored_one, tile_one, WIDE // BLK)

    def first(k):
        @pl.when(k != AT[0, 0])
        def _():
            act_copy(act, k, zh_peer).wait_recv()

        @pl.when(k == AT[1, 0])
        def _():
            for copy in act_forwards():
                copy.start()

        for n in range(WIDE // NARROW):
            cols = pl.ds(n * NARROW, NARROW)
            part_one[k, :, cols] = jnp.dot(rows_in[k], tile_one[:, cols], preferred_element_type=jnp.float32)
        core_copy(k).start()

    def sum_core(k):
        core_copy(k).wait_recv()
        x_out[k] = (part_one[k, my_half] + core_in[k]).astype(jnp.bfloat16)
        for d in (1, 3, 2):
            x_copy(k, d).start()
        x_own[k] = part_one[k, mine] + core_in[k, pl.ds(pl.multiple_of(x * PIECE, PIECE), PIECE)]

    def sum_x(k):
        for d in (1, 3, 2):
            x_copy(k, d).wait_recv()
        total = x_own[k]
        for d in range(3):
            total += x_in[k, d].astype(jnp.float32)
        z_out[k] = total.astype(z_out.dtype)
        for d in (1, 3, 2):
            z_copy(k, d).start()
        z_sum[k] = total

    def sum_z(k):
        for d in (1, 3, 2):
            z_copy(k, d).wait_recv()
        total = z_sum[k, :, my_cols]
        for d in range(3):
            total += z_in[k, d].astype(jnp.float32)
        hidden[k, mine, my_cols] = jnp.maximum(total + BIAS, 0.0).astype(jnp.bfloat16)
        for d in (1, 3, 2):
            hz_copy(k, d).start()

    def spread_x(k):
        for d in (1, 3, 2):
            hz_copy(k, d).wait_recv()
        for d in (1, 3, 2):
            hx_copy(k, d).start()

    def spread_core(k):
        for d in (1, 3, 2):
            hx_copy(k, d).wait_recv()
        hc_copy(k).start()

    def second(k):
        @pl.when(k == 0)
        def _():
            build(1, stored_two, tile_two, NARROW // BLK)

        hc_copy(k).wait_recv()
        part_two[...] = jnp.dot(hidden[k], tile_two[...], preferred_element_type=jnp.float32)
        for step, (half, d) in enumerate(ORDER):

            @pl.when(k == step)
            def _():
                if d:
                    y_out[half, d - 1] = part_two[...].astype(jnp.bfloat16)
                    y_copy(half, d).start()
                else:
                    kept[half] = part_two[...]

    def share_sum(half):
        total = kept[half]
        for d in range(3):
            total += y_in[half, d].astype(jnp.float32)
        return total

    def sum_other(k):
        @pl.when(k == LAST_OTHER)
        def _():
            for d in (1, 3, 2):
                y_copy(1, d).wait_recv()
            zh_out[...] = share_sum(1).astype(zh_out.dtype)
            zh_copy().start()

    stages = dict(
        first=first, sum_core=sum_core, sum_x=sum_x, sum_z=sum_z,
        spread_x=spread_x, spread_core=spread_core, second=second, sum_other=sum_other,
    )

    def step(t, _):
        for name, lag in PLAN:
            k = t - lag

            @pl.when((k >= 0) & (k < CHUNKS))
            def _():
                stages[name](k)

        return 0

    lax.fori_loop(0, CHUNKS + max(lag for _, lag in PLAN), step, 0)

    for d in (1, 3, 2):
        y_copy(0, d).wait_recv()
    zh_copy().wait_recv()
    total = share_sum(0) + zh_in[...].astype(jnp.float32)
    out[...] = jnp.maximum(total + BIAS, 0.0).astype(jnp.bfloat16)

    def sent(k, _):
        core_copy(k).wait_send()
        hc_copy(k).wait_send()
        for d in (1, 2, 3):
            x_copy(k, d).wait_send()
            z_copy(k, d).wait_send()
            hz_copy(k, d).wait_send()
            hx_copy(k, d).wait_send()
        return 0

    lax.fori_loop(0, CHUNKS, sent, 0)
    for copy in (*act_sends(), *act_forwards(), *(y_copy(half, d) for half in (0, 1) for d in (1, 2, 3)), zh_copy()):
        copy.wait_send()


def fused(table, act, blocks_one, blocks_two):
    bf16, f32 = jnp.bfloat16, jnp.float32
    dma = pltpu.SemaphoreType.DMA
    whole = pl.BlockSpec(memory_space=pltpu.VMEM)
    apart = pl.BlockSpec(memory_space=pl.ANY)
    scratch = [
        pltpu.VMEM((SLOTS + 1, BLK, BLK), bf16),
        pltpu.VMEM((SLOTS + 1, BLK, BLK), bf16),
        pltpu.VMEM((NARROW, WIDE), bf16),
        pltpu.VMEM((WIDE, NARROW), bf16),
        pltpu.VMEM((CHUNKS, ROWS, NARROW), bf16),
        pltpu.VMEM((CHUNKS, ROWS, WIDE), f32),
        pltpu.VMEM((CHUNKS, HALF, WIDE), f32),
        pltpu.VMEM((CHUNKS, HALF, WIDE), bf16),
        pltpu.VMEM((CHUNKS, 3, PIECE, WIDE), bf16),
        pltpu.VMEM((CHUNKS, PIECE, WIDE), f32),
        pltpu.VMEM((CHUNKS, PIECE, WIDE), f32),
        pltpu.VMEM((CHUNKS, PIECE, WIDE), Z_TYPE),
        pltpu.VMEM((CHUNKS, 3, PIECE, NARROW), Z_TYPE),
        pltpu.VMEM((CHUNKS, ROWS, WIDE), bf16),
        pltpu.VMEM((ROWS, NARROW), f32),
        pltpu.VMEM((2, ROWS, NARROW), f32),
        pltpu.VMEM((2, 3, ROWS, NARROW), bf16),
        pltpu.VMEM((2, 3, ROWS, NARROW), bf16),
        pltpu.VMEM((ROWS, NARROW), bf16),
        pltpu.VMEM((ROWS, NARROW), bf16),
        dma((2,)),
    ]
    for shape in ((CHUNKS,), (CHUNKS,), (CHUNKS, 3), (CHUNKS, 3), (CHUNKS, 3), (CHUNKS, 3), (CHUNKS,), (2, 3), ()):
        scratch += [dma(shape), dma(shape)]
    return pl.pallas_call(
        kernel,
        name="fused_layers",
        out_shape=jax.ShapeDtypeStruct((ROWS, NARROW), bf16),
        in_specs=[pl.BlockSpec(memory_space=pltpu.SMEM), whole, apart, apart],
        out_specs=whole,
        scratch_shapes=scratch,
        compiler_params=pltpu.CompilerParams(collective_id=0, has_side_effects=True, vmem_limit_bytes=56 << 20),
    )(table, act, blocks_one, blocks_two)


def slot_at(pattern, count):
    where, live = pattern.reshape(-1), count.reshape(())
    slots = jnp.arange(SLOTS, dtype=jnp.int32)
    hit = (slots[:, None] == where[None, :]) & (slots < live)[None, :]
    return jnp.min(jnp.where(hit, slots[None, :], SLOTS), axis=1)


def shards(activations, blocks_one, pattern_one, count_one, blocks_two, pattern_two, count_two):
    table = jnp.stack([slot_at(pattern_one, count_one), slot_at(pattern_two, count_two)])
    return fused(
        table, activations, blocks_one.reshape(SLOTS, BLK, BLK), blocks_two.reshape(SLOTS, BLK, BLK)
    )


def solution(mesh):
    return jax.shard_map(
        shards,
        mesh=mesh,
        in_specs=(
            P("col", "row"),
            P("row", "col", None, None, None),
            P("row", "col", None),
            P("row", "col"),
            P("col", "row", None, None, None),
            P("col", "row", None),
            P("col", "row"),
        ),
        out_specs=P("col", "row"),
        check_vma=False,
    )
```

time: 306 us -> 117 us (0.38)
  the two profiles are of different devices: /device:TPU:32 before, /device:TPU:1 now
where the time goes in v1:
time: 117 us
  Pallas kernels  112 us (96%)
  other arithmetic  2.14 us (2%)
  local copies, waits for them, and re-layouts  1.57 us (1%)
  between operations  1.33 us (1%)
    pallas_call x1, Pallas kernels, fused(): pl.pallas_call(kernel, name='fused_layers', out_shape=jax.ShapeDtypeStruc...  112 us

profile of v1, /device:TPU:1, one launch (start us, length us, event | category | flops | bytes accessed | tf_op | source)
XLA Modules:
  0.0 116.7 jit_solution(15742978173582302810)
XLA Ops:
  1.3 0.8 select_reduce_fusion
  2.1 0.8 select_reduce_fusion.1
  2.9 0.6 pad_add_fusion.table
  3.5 111.7 %fused_layers.1 = bf16[128,512]{1,0:T(8,128)(2,1)} custom-call(s32[2,64]{1,0:T(2,128)} %pad_add_fusion.table, bf16[128,512]{1,0:T(8,128)(2,1)} %act.1, bf16[64,128,128]{2,1,0:T(8,128)(2,1)} %bitcast.10, bf16[64,128,128]{2,1,0:T(8,128)(2,1)} %bitcast.11), custom_call_target="tpu_custom_call" | custom-call | tf_op jit(solution)/shard_map/fused_layers/pallas_call | solution.py:291
  115.1 1.6 %copy.11 = bf16[128,512]{1,0:T(8,128)(2,1)} copy(bf16[128,512]{1,0:T(8,128)(2,1)} %fused_layers.1) | data formatting | bytes 262144
  (2 shorter events, 0.0 us)

commit v2 on v1

v2 whole, which is shorter than its diff:
```python
import jax
import jax.numpy as jnp
from jax import lax
from jax.experimental import pallas as pl
from jax.experimental.pallas import tpu as pltpu
from jax.sharding import PartitionSpec as P

MESH = pl.DeviceIdType.MESH
BIAS = -0.3
BLK = 128
SLOTS = 64
LANES = 128
ROWS = 128
WIDE = 2048
NARROW = 512
CHUNKS = 8
HALF, PIECE = ROWS // 2, ROWS // 8
ORDER = (
    (1, 2), (0, 3), (0, 0), (0, 1), (0, 2), (1, 0), (1, 1), (1, 3),
)
AT = {step: k for k, step in enumerate(ORDER)}
STAGES = (
    "first",
    "sum_core",
    "relay",
    "sum_x",
    "sum_z",
    "spread_x",
    "pass_x",
    "spread_core",
    "second",
    "sum_other",
    "build_two",
)
SCHEDULE = (
    2, 3, 10, 1, 11, 5, 9, 80, 19, 13, 17, 7, 6, 21, 18, 27,
    15, 0, 14, 4, 25, 23, 8, 35, 22, 29, 31, 16, 12, 43, 30, 24,
    39, 20, 38, 32, 28, 51, 47, 46, 33, 40, 37, 26, 55, 54, 59, 36,
    48, 41, 63, 62, 45, 71, 70, 56, 44, 34, 53, 49, 64, 52, 67, 61,
    57, 60, 69, 72, 42, 68, 50, 65, 58, 66,
)
STEP = (1, 3)
SIDE = (pl.ds(0, WIDE // 2), pl.ds(WIDE // 2, WIDE // 2))
Z_TYPE = jnp.bfloat16


PACK, CODES = 4, 128
IDLE = CODES - 1
WORDS = []
for _start in range(0, len(SCHEDULE), PACK):
    _codes = (SCHEDULE[_start : _start + PACK] + (IDLE,) * PACK)[:PACK]
    WORDS.append(sum(code * CODES**n for n, code in enumerate(_codes)))


def kernel(
    act, blocks_one, pattern_one, count_one, blocks_two, pattern_two, count_two, out,
    stored_one, stored_two, tile_one, tile_two, rows_in, part_one, core_in, x_out, far_in, near_in, relay_out, relay_in, z_sum, z_out, z_in, hidden,
    part_two, kept, y_out, y_in, zh_out, zh_in,
    found, table, load_sem, act_send, act_recv, core_send, core_recv, far_send, far_recv, near_send, near_recv, relay_send, relay_recv, z_send, z_recv,
    hz_send, hz_recv, hx_send, hx_recv, pass_send, pass_recv, hc_send, hc_recv, y_send, y_recv, zh_send, zh_recv,
):
    row, col = lax.axis_index("row"), lax.axis_index("col")
    zl, x, core = row // 8, (row // 2) % 4, row % 2
    zh, y = col // 4, col % 4

    def row_at(zl, x, core):
        return ((zl * 4 + x) * 2 + core, col)

    other_core = row_at(zl, x, 1 - core)
    x_peer = [row_at(zl, (x + d) % 4, core) for d in range(4)]
    z_peer = [row_at((zl + d) % 4, x, core) for d in range(4)]
    y_peer = [(row, zh * 4 + (y + d) % 4) for d in range(4)]
    zh_peer = (row, (1 - zh) * 4 + y)

    def send(src, dst, send_sem, recv_sem, device):
        return pltpu.make_async_remote_copy(
            src_ref=src, dst_ref=dst, send_sem=send_sem, recv_sem=recv_sem,
            device_id=device, device_id_type=MESH,
        )

    def act_copy(src, k, device):
        return send(src, rows_in.at[k], act_send.at[k], act_recv.at[k], device)

    def core_copy(k):
        src = part_one.at[k, pl.ds(pl.multiple_of((1 - core) * HALF, HALF), HALF)]
        return send(src, core_in.at[k], core_send.at[k], core_recv.at[k], other_core)

    def rows_of(step):
        return pl.ds(pl.multiple_of((x + step) % 4 * PIECE, PIECE), PIECE)

    def far_copy(k, way):
        src = x_out.at[k, rows_of(2), SIDE[way]]
        return send(src, far_in.at[k, way], far_send.at[k, way], far_recv.at[k, way], x_peer[STEP[way]])

    def near_copy(k, way):
        src = x_out.at[k, rows_of(STEP[way]), SIDE[1 - way]]
        return send(src, near_in.at[k, way], near_send.at[k, way], near_recv.at[k, way], x_peer[STEP[way]])

    def relay_copy(k, way):
        src = relay_out.at[k, way]
        return send(src, relay_in.at[k, way], relay_send.at[k, way], relay_recv.at[k, way], x_peer[STEP[way]])

    def z_copy(k, d):
        src = z_out.at[k, :, pl.ds(pl.multiple_of((zl + d) % 4 * NARROW, NARROW), NARROW)]
        return send(src, z_in.at[k, d - 1], z_send.at[k, d - 1], z_recv.at[k, d - 1], z_peer[d])

    mine = pl.ds(pl.multiple_of(core * HALF + x * PIECE, PIECE), PIECE)
    my_half = pl.ds(pl.multiple_of(core * HALF, HALF), HALF)
    my_cols = pl.ds(pl.multiple_of(zl * NARROW, NARROW), NARROW)

    def hz_copy(k, d):
        ref = hidden.at[k, mine, my_cols]
        return send(ref, ref, hz_send.at[k, d - 1], hz_recv.at[k, d - 1], z_peer[d])

    def hx_copy(k, way):
        ref = hidden.at[k, mine]
        return send(ref, ref, hx_send.at[k, way], hx_recv.at[k, way], x_peer[STEP[way]])

    def pass_copy(k, way):
        behind = core * HALF + (x + STEP[1 - way]) % 4 * PIECE
        ref = hidden.at[k, pl.ds(pl.multiple_of(behind, PIECE), PIECE), SIDE[way]]
        return send(ref, ref, pass_send.at[k, way], pass_recv.at[k, way], x_peer[STEP[way]])

    def hc_copy(k):
        ref = hidden.at[k, my_half]
        return send(ref, ref, hc_send.at[k], hc_recv.at[k], other_core)

    def y_copy(half, d):
        return send(
            y_out.at[half, d - 1], y_in.at[half, d - 1], y_send.at[half, d - 1], y_recv.at[half, d - 1], y_peer[d]
        )

    def zh_copy():
        return send(zh_out, zh_in, zh_send, zh_recv, zh_peer)

    def act_sends():
        yield act_copy(act, AT[0, 1], y_peer[3])
        yield act_copy(act, AT[1, 0], zh_peer)
        for d in (1, 2):
            yield act_copy(act, AT[0, 4 - d], y_peer[d])

    def act_forwards():
        for d in (3, 1, 2):
            yield act_copy(rows_in.at[AT[1, 0]], AT[1, 4 - d], y_peer[d])

    loads = [
        pltpu.make_async_copy(ref, stored.at[pl.ds(0, SLOTS)], load_sem.at[layer])
        for layer, (ref, stored) in enumerate(((blocks_one, stored_one), (blocks_two, stored_two)))
    ]
    for load in loads:
        load.start()

    place = lax.broadcasted_iota(jnp.int32, (LANES, LANES), 0)
    slot = lax.broadcasted_iota(jnp.int32, (LANES, LANES), 1)
    for layer, (pattern, count) in enumerate(((pattern_one, count_one), (pattern_two, count_two))):
        where = jnp.concatenate([pattern[...], jnp.zeros((1, LANES - SLOTS), jnp.int32)], axis=1)
        hit = (where == place) & (slot < count[0, 0])
        found[pl.ds(layer, 1), :] = jnp.min(jnp.where(hit, slot, SLOTS).T, axis=0, keepdims=True)
    fill = pltpu.make_async_copy(found, table, load_sem.at[2])
    fill.start()

    barrier = pltpu.get_barrier_semaphore()
    partners = [other_core, zh_peer, x_peer[1], x_peer[3], *z_peer[1:], *y_peer[1:]]
    for device in partners:
        pl.semaphore_signal(barrier, inc=1, device_id=device, device_id_type=MESH)
    pl.semaphore_wait(barrier, len(partners))

    for copy in act_sends():
        copy.start()
    rows_in[AT[0, 0]] = act[...]
    fill.wait()
    for stored in (stored_one, stored_two):
        stored[SLOTS] = jnp.zeros((BLK, BLK), jnp.bfloat16)

    def build(layer, stored, tile, block_cols):
        def put(p, _):
            r = pl.multiple_of(p // block_cols * BLK, BLK)
            c = pl.multiple_of(p % block_cols * BLK, BLK)
            tile[pl.ds(r, BLK), pl.ds(c, BLK)] = stored[table[layer, p]]
            return 0

        loads[layer].wait()
        lax.fori_loop(0, SLOTS, put, 0)

    build(0, stored_one, tile_one, WIDE // BLK)

    def first(k):
        @pl.when(k != AT[0, 0])
        def _():
            act_copy(act, k, zh_peer).wait_recv()

        @pl.when(k == AT[1, 0])
        def _():
            for copy in act_forwards():
                copy.start()

        for n in range(WIDE // NARROW):
            cols = pl.ds(n * NARROW, NARROW)
            part_one[k, :, cols] = jnp.dot(rows_in[k], tile_one[:, cols], preferred_element_type=jnp.float32)
        core_copy(k).start()

    def sum_core(k):
        core_copy(k).wait_recv()
        x_out[k] = (part_one[k, my_half] + core_in[k]).astype(jnp.bfloat16)
        for way in range(2):
            far_copy(k, way).start()
        for way in range(2):
            near_copy(k, way).start()

    def own_sum(k, step, cols):
        rows = core * HALF + (x + step) % 4 * PIECE
        return part_one[k, pl.ds(pl.multiple_of(rows, PIECE), PIECE), cols] + core_in[k, rows_of(step), cols]

    def relay(k):
        for way in range(2):
            far_copy(k, way).wait_recv()
            total = own_sum(k, STEP[way], SIDE[way]) + far_in[k, way].astype(jnp.float32)
            relay_out[k, way] = total.astype(jnp.bfloat16)
            relay_copy(k, way).start()

    def sum_x(k):
        for way in range(2):
            near_copy(k, way).wait_recv()
            relay_copy(k, way).wait_recv()
        sides = []
        for way in range(2):
            side = own_sum(k, 0, SIDE[way])
            side += near_in[k, 1 - way].astype(jnp.float32) + relay_in[k, way].astype(jnp.float32)
            sides.append(side)
        total = jnp.concatenate(sides, axis=1)
        z_out[k] = total.astype(z_out.dtype)
        for d in (1, 3, 2):
            z_copy(k, d).start()
        z_sum[k] = total

    def sum_z(k):
        for d in (1, 3, 2):
            z_copy(k, d).wait_recv()
        total = z_sum[k, :, my_cols]
        for d in range(3):
            total += z_in[k, d].astype(jnp.float32)
        hidden[k, mine, my_cols] = jnp.maximum(total + BIAS, 0.0).astype(jnp.bfloat16)
        for d in (1, 3, 2):
            hz_copy(k, d).start()

    def spread_x(k):
        for d in (1, 3, 2):
            hz_copy(k, d).wait_recv()
        for way in range(2):
            hx_copy(k, way).start()

    def pass_x(k):
        for way in range(2):
            hx_copy(k, way).wait_recv()
            pass_copy(k, way).start()

    def spread_core(k):
        for way in range(2):
            pass_copy(k, way).wait_recv()
        hc_copy(k).start()

    def second(k):
        hc_copy(k).wait_recv()
        part_two[...] = jnp.dot(hidden[k], tile_two[...], preferred_element_type=jnp.float32)
        for step, (half, d) in enumerate(ORDER):

            @pl.when(k == step)
            def _():
                if d:
                    y_out[half, d - 1] = part_two[...].astype(jnp.bfloat16)
                    y_copy(half, d).start()
                else:
                    kept[half] = part_two[...]

    def share_sum(half):
        total = kept[half]
        for d in range(3):
            total += y_in[half, d].astype(jnp.float32)
        return total

    def sum_other(k):
        for d in (1, 3, 2):
            y_copy(1, d).wait_recv()
        zh_out[...] = share_sum(1).astype(zh_out.dtype)
        zh_copy().start()

    def build_two(k):
        build(1, stored_two, tile_two, NARROW // BLK)

    here = locals()
    stages = [here[name] for name in STAGES]

    def group(n, _):
        word = jnp.int32(WORDS[0])
        for m in range(1, len(WORDS)):
            word = jnp.where(n == m, WORDS[m], word)

        def entry(_, word):
            code = lax.rem(word, CODES)
            for number, stage in enumerate(stages):

                @pl.when(lax.div(code, CHUNKS) == number)
                def _():
                    stage(lax.rem(code, CHUNKS))

            return lax.div(word, CODES)

        lax.fori_loop(0, PACK, entry, word)
        return 0

    lax.fori_loop(0, len(WORDS), group, 0)

    for d in (1, 3, 2):
        y_copy(0, d).wait_recv()
    zh_copy().wait_recv()
    out[...] = share_sum(0) + zh_in[...].astype(jnp.float32)

    def sent(k, _):
        core_copy(k).wait_send()
        hc_copy(k).wait_send()
        for way in range(2):
            for copy in (far_copy, near_copy, relay_copy, hx_copy, pass_copy):
                copy(k, way).wait_send()
        for d in (1, 2, 3):
            z_copy(k, d).wait_send()
            hz_copy(k, d).wait_send()
        return 0

    lax.fori_loop(0, CHUNKS, sent, 0)
    for copy in (*act_sends(), *act_forwards(), *(y_copy(half, d) for half in (0, 1) for d in (1, 2, 3)), zh_copy()):
        copy.wait_send()


def fused(act, blocks_one, pattern_one, count_one, blocks_two, pattern_two, count_two):
    bf16, f32 = jnp.bfloat16, jnp.float32
    dma = pltpu.SemaphoreType.DMA
    whole = pl.BlockSpec(memory_space=pltpu.VMEM)
    scalar = pl.BlockSpec(memory_space=pltpu.SMEM)
    apart = pl.BlockSpec(memory_space=pl.ANY)
    scratch = [
        pltpu.VMEM((SLOTS + 1, BLK, BLK), bf16),
        pltpu.VMEM((SLOTS + 1, BLK, BLK), bf16),
        pltpu.VMEM((NARROW, WIDE), bf16),
        pltpu.VMEM((WIDE, NARROW), bf16),
        pltpu.VMEM((CHUNKS, ROWS, NARROW), bf16),
        pltpu.VMEM((CHUNKS, ROWS, WIDE), f32),
        pltpu.VMEM((CHUNKS, HALF, WIDE), f32),
        pltpu.VMEM((CHUNKS, HALF, WIDE), bf16),
        pltpu.VMEM((CHUNKS, 2, PIECE, WIDE // 2), bf16),
        pltpu.VMEM((CHUNKS, 2, PIECE, WIDE // 2), bf16),
        pltpu.VMEM((CHUNKS, 2, PIECE, WIDE // 2), bf16),
        pltpu.VMEM((CHUNKS, 2, PIECE, WIDE // 2), bf16),
        pltpu.VMEM((CHUNKS, PIECE, WIDE), f32),
        pltpu.VMEM((CHUNKS, PIECE, WIDE), Z_TYPE),
        pltpu.VMEM((CHUNKS, 3, PIECE, NARROW), Z_TYPE),
        pltpu.VMEM((CHUNKS, ROWS, WIDE), bf16),
        pltpu.VMEM((ROWS, NARROW), f32),
        pltpu.VMEM((2, ROWS, NARROW), f32),
        pltpu.VMEM((2, 3, ROWS, NARROW), bf16),
        pltpu.VMEM((2, 3, ROWS, NARROW), bf16),
        pltpu.VMEM((ROWS, NARROW), bf16),
        pltpu.VMEM((ROWS, NARROW), bf16),
        pltpu.VMEM((2, LANES), jnp.int32),
        pltpu.SMEM((2, LANES), jnp.int32),
        dma((3,)),
    ]
    one, two, three = (CHUNKS,), (CHUNKS, 2), (CHUNKS, 3)
    for shape in (one, one, two, two, two, three, three, two, two, one, (2, 3), ()):
        scratch += [dma(shape), dma(shape)]
    return pl.pallas_call(
        kernel,
        name="fused_layers",
        out_shape=jax.ShapeDtypeStruct((ROWS, NARROW), f32),
        in_specs=[whole, apart, whole, scalar, apart, whole, scalar],
        out_specs=whole,
        scratch_shapes=scratch,
        compiler_params=pltpu.CompilerParams(collective_id=0, has_side_effects=True, vmem_limit_bytes=56 << 20),
    )(act, blocks_one, pattern_one, count_one, blocks_two, pattern_two, count_two)


def shards(activations, blocks_one, pattern_one, count_one, blocks_two, pattern_two, count_two):
    total = fused(
        activations,
        blocks_one.reshape(SLOTS, BLK, BLK),
        pattern_one.reshape(1, SLOTS),
        count_one,
        blocks_two.reshape(SLOTS, BLK, BLK),
        pattern_two.reshape(1, SLOTS),
        count_two,
    )
    return jnp.maximum(total + BIAS, 0.0).astype(jnp.bfloat16)


def solution(mesh):
    return jax.shard_map(
        shards,
        mesh=mesh,
        in_specs=(
            P("col", "row"),
            P("row", "col", None, None, None),
            P("row", "col", None),
            P("row", "col"),
            P("col", "row", None, None, None),
            P("col", "row", None),
            P("col", "row"),
        ),
        out_specs=P("col", "row"),
        check_vma=False,
    )
```

time: 117 us -> 79.9 us (0.68)
  Pallas kernels: 112 us -> 76.8 us
  local copies, waits for them, and re-layouts: 1.57 us -> 0 us
    pallas_call x1, Pallas kernels: 112 us -> 76.8 us  [fused(): pl.pallas_call(kernel, name='fused_layers', out_shape=jax.ShapeDtypeStruc...]
    convert_element_type x0 -> x1, other arithmetic: none -> 1.63 us  [shards(): return jnp.maximum(total + BIAS, 0.0).astype(jnp.bfloat16)]
    unnamed x1 -> x0, local copies, waits for them, and re-layouts: 1.57 us -> none
    reduce_min x2 -> x0, other arithmetic: 1.55 us -> none  [slot_at(): return jnp.min(jnp.where(hit, slots[None, :], SLOTS), axis=1)]
where the time goes in v2:
time: 79.9 us; the launch traced here: 79.8 us
  Pallas kernels  76.8 us (96%)
  other arithmetic  1.63 us (2%)
  between operations  1.3 us (2%)
    pallas_call x1, Pallas kernels, fused(): pl.pallas_call(kernel, name='fused_layers', out_shape=jax.ShapeDtypeStruc...  76.8 us
    convert_element_type x1, other arithmetic, shards(): return jnp.maximum(total + BIAS, 0.0).astype(jnp.bfloat16)  1.63 us

profile of v2, /device:TPU:1, one launch (start us, length us, event | category | flops | bytes accessed | tf_op | source)
XLA Modules:
  0.0 79.8 jit_solution(5391302799299300306)
XLA Ops:
  1.3 76.8 %fused_layers.1 = f32[128,512]{1,0:T(8,128)} custom-call(bf16[128,512]{1,0:T(8,128)(2,1)} %act.1, bf16[64,128,128]{2,1,0:T(8,128)(2,1)} %bitcast.4, s32[1,64]{1,0:T(1,128)} %bitcast.6, s32[1,1]{1,0:T(1,128)S(6)} %copy.8.count_one, bf16[64,128,128]{2,1,0:T(8,128)(2,1)} %bitcast.5, s32[1,64]{1,0:T(1,128)} %bitcast.7, s32[1,1]{1,0:T(1,128)S(6)} %copy.9.count_two), custom_call_target="tpu_custom_call" | custom-call | tf_op jit(solution)/shard_map/fused_layers/pallas_call | solution.py:370
  78.1 1.6 %maximum_convert_fusion = bf16[128,512]{1,0:T(8,128)(2,1)} fusion(f32[128,512]{1,0:T(8,128)} %fused_layers.1), kind=kLoop, calls=%fused_computation | loop fusion | flops 196608 | bytes 393216 | tf_op jit(solution)/shard_map/convert_element_type | solution.py:391

commit v3 on v2

--- a/solution.py
+++ b/solution.py
@@ -16,7 +16,7 @@
 CHUNKS = 8
 HALF, PIECE = ROWS // 2, ROWS // 8
 ORDER = (
-    (1, 2), (0, 3), (0, 0), (0, 1), (0, 2), (1, 0), (1, 1), (1, 3),
+    (0, 0), (1, 1), (1, 0), (0, 1), (0, 2), (1, 3), (1, 2), (0, 3),
 )
 AT = {step: k for k, step in enumerate(ORDER)}
 STAGES = (
@@ -31,15 +31,17 @@
     "second",
     "sum_other",
     "build_two",
+    "forward",
 )
 SCHEDULE = (
-    2, 3, 10, 1, 11, 5, 9, 80, 19, 13, 17, 7, 6, 21, 18, 27,
-    15, 0, 14, 4, 25, 23, 8, 35, 22, 29, 31, 16, 12, 43, 30, 24,
-    39, 20, 38, 32, 28, 51, 47, 46, 33, 40, 37, 26, 55, 54, 59, 36,
-    48, 41, 63, 62, 45, 71, 70, 56, 44, 34, 53, 49, 64, 52, 67, 61,
-    57, 60, 69, 72, 42, 68, 50, 65, 58, 66,
+    80, 0, 3, 88, 11, 4, 89, 8, 2, 19, 7, 12, 5, 10, 27, 6,
+    13, 1, 18, 14, 21, 9, 35, 22, 26, 29, 17, 16, 43, 30, 34, 15,
+    20, 25, 38, 51, 42, 37, 23, 33, 28, 46, 45, 31, 41, 54, 36, 50,
+    53, 39, 49, 24, 62, 44, 58, 61, 70, 57, 47, 59, 69, 32, 52, 65,
+    67, 55, 66, 40, 60, 72, 68, 73, 63, 48, 71, 56, 64,
 )
 STEP = (1, 3)
+PART = (pl.ds(0, NARROW // 2), pl.ds(NARROW // 2, NARROW // 2))
 SIDE = (pl.ds(0, WIDE // 2), pl.ds(WIDE // 2, WIDE // 2))
 Z_TYPE = jnp.bfloat16
 
@@ -54,6 +56,7 @@
 
 def kernel(
     act, blocks_one, pattern_one, count_one, blocks_two, pattern_two, count_two, out,
+    patterns, counts,
     stored_one, stored_two, tile_one, tile_two, rows_in, part_one, core_in, x_out, far_in, near_in, relay_out, relay_in, z_sum, z_out, z_in, hidden,
     part_two, kept, y_out, y_in, zh_out, zh_in,
     found, table, load_sem, act_send, act_recv, core_send, core_recv, far_send, far_recv, near_send, near_recv, relay_send, relay_recv, z_send, z_recv,
@@ -78,8 +81,9 @@
             device_id=device, device_id_type=MESH,
         )
 
-    def act_copy(src, k, device):
-        return send(src, rows_in.at[k], act_send.at[k], act_recv.at[k], device)
+    def act_copy(src, k, piece, device):
+        rows = pl.ds(pl.multiple_of(piece * HALF, HALF), HALF)
+        return send(src.at[rows], rows_in.at[k, rows], act_send.at[k, piece], act_recv.at[k, piece], device)
 
     def core_copy(k):
         src = part_one.at[k, pl.ds(pl.multiple_of((1 - core) * HALF, HALF), HALF)]
@@ -125,52 +129,68 @@
         ref = hidden.at[k, my_half]
         return send(ref, ref, hc_send.at[k], hc_recv.at[k], other_core)
 
-    def y_copy(half, d):
-        return send(
-            y_out.at[half, d - 1], y_in.at[half, d - 1], y_send.at[half, d - 1], y_recv.at[half, d - 1], y_peer[d]
+    def y_copy(half, d, piece):
+        at = (half, d - 1, piece)
+        return send(y_out.at[at], y_in.at[at], y_send.at[at], y_recv.at[at], (row, zh * 4 + (y + d) % 4))
+
+    def zh_copy(piece):
+        return send(zh_out.at[piece], zh_in.at[piece], zh_send.at[piece], zh_recv.at[piece], zh_peer)
+
+    def act_sends():
+        for piece in range(2):
+            yield act_copy(rows_in.at[AT[0, 0]], AT[1, 0], piece, zh_peer)
+        for d in (3, 1, 2):
+            for piece in range(2):
+                yield act_copy(rows_in.at[AT[0, 0]], AT[0, 4 - d], piece, y_peer[d])
+
+    def act_forwards(piece):
+        for d in (3, 1, 2):
+            yield act_copy(rows_in.at[AT[1, 0]], AT[1, 4 - d], piece, y_peer[d])
+
+    barrier = pltpu.get_barrier_semaphore()
+    partners = [other_core, zh_peer, x_peer[1], x_peer[3], *z_peer[1:], *y_peer[1:]]
+    for device in partners:
+        pl.semaphore_signal(barrier, inc=1, device_id=device, device_id_type=MESH)
+
+    own = AT[0, 0]
+    own_load = pltpu.make_async_copy(act, rows_in.at[own], load_sem.at[3])
+    facts = [
+        pltpu.make_async_copy(src, dst, load_sem.at[n])
+        for n, (src, dst) in enumerate(
+            (
+                (pattern_one, patterns.at[0]),
+                (pattern_two, patterns.at[1]),
+                (count_one, counts.at[0]),
+                (count_two, counts.at[1]),
+            ),
+            start=4,
         )
-
-    def zh_copy():
-        return send(zh_out, zh_in, zh_send, zh_recv, zh_peer)
-
-    def act_sends():
-        yield act_copy(act, AT[0, 1], y_peer[3])
-        yield act_copy(act, AT[1, 0], zh_peer)
-        for d in (1, 2):
-            yield act_copy(act, AT[0, 4 - d], y_peer[d])
-
-    def act_forwards():
-        for d in (3, 1, 2):
-            yield act_copy(rows_in.at[AT[1, 0]], AT[1, 4 - d], y_peer[d])
-
+    ]
     loads = [
         pltpu.make_async_copy(ref, stored.at[pl.ds(0, SLOTS)], load_sem.at[layer])
         for layer, (ref, stored) in enumerate(((blocks_one, stored_one), (blocks_two, stored_two)))
     ]
-    for load in loads:
+    for load in (own_load, *facts, *loads):
         load.start()
+    for stored in (stored_one, stored_two):
+        stored[SLOTS] = jnp.zeros((BLK, BLK), jnp.bfloat16)
+    for fact in facts:
+        fact.wait()
 
     place = lax.broadcasted_iota(jnp.int32, (LANES, LANES), 0)
     slot = lax.broadcasted_iota(jnp.int32, (LANES, LANES), 1)
-    for layer, (pattern, count) in enumerate(((pattern_one, count_one), (pattern_two, count_two))):
-        where = jnp.concatenate([pattern[...], jnp.zeros((1, LANES - SLOTS), jnp.int32)], axis=1)
-        hit = (where == place) & (slot < count[0, 0])
+    for layer in range(2):
+        where = jnp.concatenate([patterns[layer], jnp.zeros((1, LANES - SLOTS), jnp.int32)], axis=1)
+        hit = (where == place) & (slot < counts[layer, 0, 0])
         found[pl.ds(layer, 1), :] = jnp.min(jnp.where(hit, slot, SLOTS).T, axis=0, keepdims=True)
     fill = pltpu.make_async_copy(found, table, load_sem.at[2])
     fill.start()
-
-    barrier = pltpu.get_barrier_semaphore()
-    partners = [other_core, zh_peer, x_peer[1], x_peer[3], *z_peer[1:], *y_peer[1:]]
-    for device in partners:
-        pl.semaphore_signal(barrier, inc=1, device_id=device, device_id_type=MESH)
+    own_load.wait()
+
     pl.semaphore_wait(barrier, len(partners))
-
     for copy in act_sends():
         copy.start()
-    rows_in[AT[0, 0]] = act[...]
     fill.wait()
-    for stored in (stored_one, stored_two):
-        stored[SLOTS] = jnp.zeros((BLK, BLK), jnp.bfloat16)
 
     def build(layer, stored, tile, block_cols):
         def put(p, _):
@@ -184,15 +204,16 @@
 
     build(0, stored_one, tile_one, WIDE // BLK)
 
+    def forward(piece):
+        act_copy(rows_in.at[AT[0, 0]], AT[1, 0], piece, zh_peer).wait_recv()
+        for copy in act_forwards(piece):
+            copy.start()
+
     def first(k):
-        @pl.when(k != AT[0, 0])
+        @pl.when((k != AT[0, 0]) & (k != AT[1, 0]))
         def _():
-            act_copy(act, k, zh_peer).wait_recv()
-
-        @pl.when(k == AT[1, 0])
-        def _():
-            for copy in act_forwards():
-                copy.start()
+            for piece in range(2):
+                act_copy(rows_in.at[AT[0, 0]], k, piece, zh_peer).wait_recv()
 
         for n in range(WIDE // NARROW):
             cols = pl.ds(n * NARROW, NARROW)
@@ -261,28 +282,33 @@
 
     def second(k):
         hc_copy(k).wait_recv()
-        part_two[...] = jnp.dot(hidden[k], tile_two[...], preferred_element_type=jnp.float32)
-        for step, (half, d) in enumerate(ORDER):
-
-            @pl.when(k == step)
+        half, d = jnp.int32(ORDER[0][0]), jnp.int32(ORDER[0][1])
+        for other, steps in enumerate(ORDER):
+            half = jnp.where(k == other, steps[0], half)
+            d = jnp.where(k == other, steps[1], d)
+        for piece in range(2):
+            part_two[...] = jnp.dot(hidden[k], tile_two[:, PART[piece]], preferred_element_type=jnp.float32)
+
+            @pl.when(d == 0)
             def _():
-                if d:
-                    y_out[half, d - 1] = part_two[...].astype(jnp.bfloat16)
-                    y_copy(half, d).start()
-                else:
-                    kept[half] = part_two[...]
-
-    def share_sum(half):
-        total = kept[half]
+                kept[half, piece] = part_two[...]
+
+            @pl.when(d != 0)
+            def _():
+                y_out[half, d - 1, piece] = part_two[...].astype(jnp.bfloat16)
+                y_copy(half, d, piece).start()
+
+    def share_sum(half, piece):
+        total = kept[half, piece]
         for d in range(3):
-            total += y_in[half, d].astype(jnp.float32)
+            total += y_in[half, d, piece].astype(jnp.float32)
         return total
 
-    def sum_other(k):
-        for d in (1, 3, 2):
-            y_copy(1, d).wait_recv()
-        zh_out[...] = share_sum(1).astype(zh_out.dtype)
-        zh_copy().start()
+    def sum_other(piece):
+        for d in (1, 3, 2):
+            y_copy(1, d, piece).wait_recv()
+        zh_out[piece] = share_sum(1, piece).astype(zh_out.dtype)
+        zh_copy(piece).start()
 
     def build_two(k):
         build(1, stored_two, tile_two, NARROW // BLK)
@@ -310,10 +336,11 @@
 
     lax.fori_loop(0, len(WORDS), group, 0)
 
-    for d in (1, 3, 2):
-        y_copy(0, d).wait_recv()
-    zh_copy().wait_recv()
-    out[...] = share_sum(0) + zh_in[...].astype(jnp.float32)
+    for piece in range(2):
+        for d in (1, 3, 2):
+            y_copy(0, d, piece).wait_recv()
+        zh_copy(piece).wait_recv()
+        out[:, PART[piece]] = share_sum(0, piece) + zh_in[piece].astype(jnp.float32)
 
     def sent(k, _):
         core_copy(k).wait_send()
@@ -327,17 +354,24 @@
         return 0
 
     lax.fori_loop(0, CHUNKS, sent, 0)
-    for copy in (*act_sends(), *act_forwards(), *(y_copy(half, d) for half in (0, 1) for d in (1, 2, 3)), zh_copy()):
+    for copy in act_sends():
         copy.wait_send()
+    for piece in range(2):
+        for copy in (*act_forwards(piece), zh_copy(piece)):
+            copy.wait_send()
+        for half in range(2):
+            for d in (1, 2, 3):
+                y_copy(half, d, piece).wait_send()
 
 
 def fused(act, blocks_one, pattern_one, count_one, blocks_two, pattern_two, count_two):
     bf16, f32 = jnp.bfloat16, jnp.float32
     dma = pltpu.SemaphoreType.DMA
     whole = pl.BlockSpec(memory_space=pltpu.VMEM)
-    scalar = pl.BlockSpec(memory_space=pltpu.SMEM)
     apart = pl.BlockSpec(memory_space=pl.ANY)
     scratch = [
+        pltpu.VMEM((2, 1, SLOTS), jnp.int32),
+        pltpu.SMEM((2, 1, 1), jnp.int32),
         pltpu.VMEM((SLOTS + 1, BLK, BLK), bf16),
         pltpu.VMEM((SLOTS + 1, BLK, BLK), bf16),
         pltpu.VMEM((NARROW, WIDE), bf16),
@@ -354,24 +388,24 @@
         pltpu.VMEM((CHUNKS, PIECE, WIDE), Z_TYPE),
         pltpu.VMEM((CHUNKS, 3, PIECE, NARROW), Z_TYPE),
         pltpu.VMEM((CHUNKS, ROWS, WIDE), bf16),
-        pltpu.VMEM((ROWS, NARROW), f32),
-        pltpu.VMEM((2, ROWS, NARROW), f32),
-        pltpu.VMEM((2, 3, ROWS, NARROW), bf16),
-        pltpu.VMEM((2, 3, ROWS, NARROW), bf16),
-        pltpu.VMEM((ROWS, NARROW), bf16),
-        pltpu.VMEM((ROWS, NARROW), bf16),
+        pltpu.VMEM((ROWS, NARROW // 2), f32),
+        pltpu.VMEM((2, 2, ROWS, NARROW // 2), f32),
+        pltpu.VMEM((2, 3, 2, ROWS, NARROW // 2), bf16),
+        pltpu.VMEM((2, 3, 2, ROWS, NARROW // 2), bf16),
+        pltpu.VMEM((2, ROWS, NARROW // 2), bf16),
+        pltpu.VMEM((2, ROWS, NARROW // 2), bf16),
         pltpu.VMEM((2, LANES), jnp.int32),
         pltpu.SMEM((2, LANES), jnp.int32),
-        dma((3,)),
+        dma((8,)),
     ]
     one, two, three = (CHUNKS,), (CHUNKS, 2), (CHUNKS, 3)
-    for shape in (one, one, two, two, two, three, three, two, two, one, (2, 3), ()):
+    for shape in (two, one, two, two, two, three, three, two, two, one, (2, 3, 2), (2,)):
         scratch += [dma(shape), dma(shape)]
     return pl.pallas_call(
         kernel,
         name="fused_layers",
         out_shape=jax.ShapeDtypeStruct((ROWS, NARROW), f32),
-        in_specs=[whole, apart, whole, scalar, apart, whole, scalar],
+        in_specs=[apart] * 7,
         out_specs=whole,
         scratch_shapes=scratch,
         compiler_params=pltpu.CompilerParams(collective_id=0, has_side_effects=True, vmem_limit_bytes=56 << 20),

time: 79.9 us -> 77 us (0.964)
  Pallas kernels: 76.8 us -> 73.9 us
    pallas_call x1, Pallas kernels: 76.8 us -> 73.9 us  [fused(): pl.pallas_call(kernel, name='fused_layers', out_shape=jax.ShapeDtypeStruc...]
where the time goes in v3:
time: 77 us; the launch traced here: 76.8 us
  Pallas kernels  73.9 us (96%)
  other arithmetic  1.63 us (2%)
  between operations  1.3 us (2%)
    pallas_call x1, Pallas kernels, fused(): pl.pallas_call(kernel, name='fused_layers', out_shape=jax.ShapeDtypeStruc...  73.9 us
    convert_element_type x1, other arithmetic, shards(): return jnp.maximum(total + BIAS, 0.0).astype(jnp.bfloat16)  1.63 us

profile of v3, /device:TPU:1, one launch (start us, length us, event | category | flops | bytes accessed | tf_op | source)
XLA Modules:
  0.0 76.8 jit_solution(11077604627825340431)
XLA Ops:
  1.3 73.9 %fused_layers.1 = f32[128,512]{1,0:T(8,128)} custom-call(bf16[128,512]{1,0:T(8,128)(2,1)} %act.1, bf16[64,128,128]{2,1,0:T(8,128)(2,1)} %bitcast.4, s32[1,64]{1,0:T(1,128)} %bitcast.6, s32[1,1]{1,0:T(1,128)S(6)} %copy.8.count_one, bf16[64,128,128]{2,1,0:T(8,128)(2,1)} %bitcast.5, s32[1,64]{1,0:T(1,128)} %bitcast.7, s32[1,1]{1,0:T(1,128)S(6)} %copy.9.count_two), custom_call_target="tpu_custom_call" | custom-call | tf_op jit(solution)/shard_map/fused_layers/pallas_call | solution.py:404
  75.2 1.6 %maximum_convert_fusion = bf16[128,512]{1,0:T(8,128)(2,1)} fusion(f32[128,512]{1,0:T(8,128)} %fused_layers.1), kind=kLoop, calls=%fused_computation | loop fusion | flops 196608 | bytes 393216 | tf_op jit(solution)/shard_map/convert_element_type | solution.py:425

commit v4 on v3

--- a/solution.py
+++ b/solution.py
@@ -408,18 +408,18 @@
         in_specs=[apart] * 7,
         out_specs=whole,
         scratch_shapes=scratch,
-        compiler_params=pltpu.CompilerParams(collective_id=0, has_side_effects=True, vmem_limit_bytes=56 << 20),
+        compiler_params=pltpu.CompilerParams(collective_id=0, has_side_effects=True, vmem_limit_bytes=53 << 20),
     )(act, blocks_one, pattern_one, count_one, blocks_two, pattern_two, count_two)
 
 
 def shards(activations, blocks_one, pattern_one, count_one, blocks_two, pattern_two, count_two):
     total = fused(
-        activations,
+        pltpu.with_memory_space_constraint(activations, pltpu.MemorySpace.HBM),
         blocks_one.reshape(SLOTS, BLK, BLK),
-        pattern_one.reshape(1, SLOTS),
+        pltpu.with_memory_space_constraint(pattern_one.reshape(1, SLOTS), pltpu.MemorySpace.HBM),
         count_one,
         blocks_two.reshape(SLOTS, BLK, BLK),
-        pattern_two.reshape(1, SLOTS),
+        pltpu.with_memory_space_constraint(pattern_two.reshape(1, SLOTS), pltpu.MemorySpace.HBM),
         count_two,
     )
     return jnp.maximum(total + BIAS, 0.0).astype(jnp.bfloat16)

time: 77 us -> 75.3 us (0.978)
  other arithmetic: 1.63 us -> 0.68 us
    convert_element_type x1, other arithmetic: 1.63 us -> 0.68 us  [shards(): return jnp.maximum(total + BIAS, 0.0).astype(jnp.bfloat16)]
where the time goes in v4:
time: 75.3 us; the launch traced here: 75.2 us
  Pallas kernels  73.2 us (97%)
  between operations  1.3 us (2%)
    pallas_call x1, Pallas kernels, fused(): pl.pallas_call(kernel, name='fused_layers', out_shape=jax.ShapeDtypeStruc...  73.2 us

profile of v4, /device:TPU:1, one launch (start us, length us, event | category | flops | bytes accessed | tf_op | source)
XLA Modules:
  0.0 75.2 jit_solution(18243140881214132402)
XLA Ops:
  1.3 73.2 %fused_layers.1 = f32[128,512]{1,0:T(8,128)S(1)} custom-call(bf16[128,512]{1,0:T(8,128)(2,1)} %act.1, bf16[64,128,128]{2,1,0:T(8,128)(2,1)} %bitcast.4, s32[1,64]{1,0:T(1,128)} %bitcast.6, s32[1,1]{1,0:T(1,128)S(6)} %copy.8.count_one, bf16[64,128,128]{2,1,0:T(8,128)(2,1)} %bitcast.5, s32[1,64]{1,0:T(1,128)} %bitcast.7, s32[1,1]{1,0:T(1,128)S(6)} %copy.9.count_two), custom_call_target="tpu_custom_call" | custom-call | tf_op jit(solution)/shard_map/fused_layers/pallas_call | solution.py:404
  74.5 0.7 maximum_convert_fusion

commit v5 on v4

--- a/solution.py
+++ b/solution.py
@@ -16,7 +16,7 @@
 CHUNKS = 8
 HALF, PIECE = ROWS // 2, ROWS // 8
 ORDER = (
-    (0, 0), (1, 1), (1, 0), (0, 1), (0, 2), (1, 3), (1, 2), (0, 3),
+    (1, 3), (1, 2), (0, 0), (0, 1), (0, 2), (0, 3), (1, 1), (1, 0),
 )
 AT = {step: k for k, step in enumerate(ORDER)}
 STAGES = (
@@ -34,11 +34,11 @@
     "forward",
 )
 SCHEDULE = (
-    80, 0, 3, 88, 11, 4, 89, 8, 2, 19, 7, 12, 5, 10, 27, 6,
-    13, 1, 18, 14, 21, 9, 35, 22, 26, 29, 17, 16, 43, 30, 34, 15,
-    20, 25, 38, 51, 42, 37, 23, 33, 28, 46, 45, 31, 41, 54, 36, 50,
-    53, 39, 49, 24, 62, 44, 58, 61, 70, 57, 47, 59, 69, 32, 52, 65,
-    67, 55, 66, 40, 60, 72, 68, 73, 63, 48, 71, 56, 64,
+    80, 2, 5, 88, 10, 89, 13, 7, 4, 15, 6, 21, 1, 23, 14, 0,
+    29, 9, 31, 8, 3, 17, 37, 22, 39, 16, 12, 25, 11, 30, 18, 47,
+    24, 20, 33, 19, 45, 38, 32, 55, 28, 41, 26, 46, 27, 40, 36, 49,
+    54, 53, 35, 48, 57, 44, 34, 62, 65, 56, 43, 70, 52, 64, 42, 63,
+    51, 61, 60, 71, 72, 68, 59, 73, 50, 69, 67, 58, 66,
 )
 STEP = (1, 3)
 PART = (pl.ds(0, NARROW // 2), pl.ds(NARROW // 2, NARROW // 2))
@@ -323,12 +323,17 @@
 
         def entry(_, word):
             code = lax.rem(word, CODES)
-            for number, stage in enumerate(stages):
-
-                @pl.when(lax.div(code, CHUNKS) == number)
-                def _():
-                    stage(lax.rem(code, CHUNKS))
-
+            number, k = lax.div(code, CHUNKS), lax.rem(code, CHUNKS)
+
+            def choose(low, high):
+                if high - low == 1:
+                    stages[low](k)
+                    return
+                middle = (low + high) // 2
+                pl.when(number < middle)(lambda: choose(low, middle))
+                pl.when(number >= middle)(lambda: choose(middle, high))
+
+            pl.when(number < len(stages))(lambda: choose(0, len(stages)))
             return lax.div(word, CODES)
 
         lax.fori_loop(0, PACK, entry, word)

time: 75.3 us -> 75.4 us (level)
  no operation moved by 1% of the time
where the time goes in v5:
time: 75.4 us; the launch traced here: 75.3 us
  Pallas kernels  73.3 us (97%)
  between operations  1.3 us (2%)
    pallas_call x1, Pallas kernels, fused(): pl.pallas_call(kernel, name='fused_layers', out_shape=jax.ShapeDtypeStruc...  73.3 us

profile of v5, /device:TPU:1, one launch (start us, length us, event | category | flops | bytes accessed | tf_op | source)
XLA Modules:
  0.0 75.3 jit_solution(3406066407610596970)
XLA Ops:
  1.3 73.3 %fused_layers.1 = f32[128,512]{1,0:T(8,128)S(1)} custom-call(bf16[128,512]{1,0:T(8,128)(2,1)} %act.1, bf16[64,128,128]{2,1,0:T(8,128)(2,1)} %bitcast.4, s32[1,64]{1,0:T(1,128)} %bitcast.6, s32[1,1]{1,0:T(1,128)S(6)} %copy.8.count_one, bf16[64,128,128]{2,1,0:T(8,128)(2,1)} %bitcast.5, s32[1,64]{1,0:T(1,128)} %bitcast.7, s32[1,1]{1,0:T(1,128)S(6)} %copy.9.count_two), custom_call_target="tpu_custom_call" | custom-call | tf_op jit(solution)/shard_map/fused_layers/pallas_call | solution.py:409
  74.6 0.7 maximum_convert_fusion

commit v6 on v5

--- a/solution.py
+++ b/solution.py
@@ -170,7 +170,7 @@
         pltpu.make_async_copy(ref, stored.at[pl.ds(0, SLOTS)], load_sem.at[layer])
         for layer, (ref, stored) in enumerate(((blocks_one, stored_one), (blocks_two, stored_two)))
     ]
-    for load in (own_load, *facts, *loads):
+    for load in (own_load, *facts, loads[0]):
         load.start()
     for stored in (stored_one, stored_two):
         stored[SLOTS] = jnp.zeros((BLK, BLK), jnp.bfloat16)
@@ -203,6 +203,7 @@
         lax.fori_loop(0, SLOTS, put, 0)
 
     build(0, stored_one, tile_one, WIDE // BLK)
+    loads[1].start()
 
     def forward(piece):
         act_copy(rows_in.at[AT[0, 0]], AT[1, 0], piece, zh_peer).wait_recv()
@@ -341,12 +342,6 @@
 
     lax.fori_loop(0, len(WORDS), group, 0)
 
-    for piece in range(2):
-        for d in (1, 3, 2):
-            y_copy(0, d, piece).wait_recv()
-        zh_copy(piece).wait_recv()
-        out[:, PART[piece]] = share_sum(0, piece) + zh_in[piece].astype(jnp.float32)
-
     def sent(k, _):
         core_copy(k).wait_send()
         hc_copy(k).wait_send()
@@ -362,11 +357,18 @@
     for copy in act_sends():
         copy.wait_send()
     for piece in range(2):
-        for copy in (*act_forwards(piece), zh_copy(piece)):
+        for copy in act_forwards(piece):
             copy.wait_send()
         for half in range(2):
             for d in (1, 2, 3):
                 y_copy(half, d, piece).wait_send()
+
+    for piece in range(2):
+        for d in (1, 3, 2):
+            y_copy(0, d, piece).wait_recv()
+        zh_copy(piece).wait_recv()
+        out[:, PART[piece]] = share_sum(0, piece) + zh_in[piece].astype(jnp.float32)
+        zh_copy(piece).wait_send()
 
 
 def fused(act, blocks_one, pattern_one, count_one, blocks_two, pattern_two, count_two):

time: 75.4 us -> 75.2 us (level)
  no operation moved by 1% of the time
where the time goes in v6:
time: 75.2 us; the launch traced here: 75 us
  Pallas kernels  73 us (97%)
  between operations  1.3 us (2%)
    pallas_call x1, Pallas kernels, fused(): pl.pallas_call(kernel, name='fused_layers', out_shape=jax.ShapeDtypeStruc...  73 us

profile of v6, /device:TPU:1, one launch (start us, length us, event | category | flops | bytes accessed | tf_op | source)
XLA Modules:
  0.0 75.0 jit_solution(8043949711549448368)
XLA Ops:
  1.3 73.0 %fused_layers.1 = f32[128,512]{1,0:T(8,128)S(1)} custom-call(bf16[128,512]{1,0:T(8,128)(2,1)} %act.1, bf16[64,128,128]{2,1,0:T(8,128)(2,1)} %bitcast.4, s32[1,64]{1,0:T(1,128)} %bitcast.6, s32[1,1]{1,0:T(1,128)S(6)} %copy.8.count_one, bf16[64,128,128]{2,1,0:T(8,128)(2,1)} %bitcast.5, s32[1,64]{1,0:T(1,128)} %bitcast.7, s32[1,1]{1,0:T(1,128)S(6)} %copy.9.count_two), custom_call_target="tpu_custom_call" | custom-call | tf_op jit(solution)/shard_map/fused_layers/pallas_call | solution.py:411
  74.4 0.7 maximum_convert_fusion
